TPU v7x, 32 devices: a whole 2x2x4 slice. The times are simulated.
32 devices in a mesh: dp: 32 (over z, y, x, core).
Axes of the slice: x: 2, y: 2, z: 4, core: 2. Of those that a mesh axis runs over, the one named last changes fastest.
Arguments:
- features: bfloat16 [32768, 768], P('dp'), may hold values from -6 to 6
- pos_conv: bfloat16 [32768, 768], P('dp'), may hold values from -3 to 3
- segment_ids: int32 [32, 1024], P('dp'), may hold values from 0 to 3, never falling along the last dimension, each value on 1 to 512 neighbouring positions
- frame_valid: int32 [32, 1024], P('dp'), may hold values 0 or 1
- cotangent: bfloat16 [32768, 768], P('dp'), may hold values from -6 to 6
- qkv_weight: float32 [768, 2304], P('dp'), may hold values from -0.21875 to 0.21875
- proj_weight: float32 [768, 768], P('dp'), may hold values from -1.75 to 1.75
- expand_weight: float32 [768, 3072], P('dp'), may hold values from -0.21875 to 0.21875
- reduce_weight: float32 [3072, 768], P('dp'), may hold values from -0.109375 to 0.109375
- norm_gains: float32 [2, 768], P(None, 'dp'), may hold values from 0.5 to 1.5
- bias_vector: float32 [7680], P('dp'), may hold values from -1.5 to 1.5
- qkv_moment: float32 [768, 2304], P('dp'), may hold values from -1086.116 to 1086.116
- proj_moment: float32 [768, 768], P('dp'), may hold values from -108.6116 to 108.6116
- expand_moment: float32 [768, 3072], P('dp'), may hold values from -325.8348 to 325.8348
- reduce_moment: float32 [3072, 768], P('dp'), may hold values from -651.6696 to 651.6696
- gains_moment: float32 [2, 768], P(None, 'dp'), may hold values from -1086.116 to 1086.116
- bias_moment: float32 [7680], P('dp'), may hold values from -1086.116 to 1086.116
- qkv_average: float32 [768, 2304], P('dp'), may hold values from -0.21875 to 0.21875
- proj_average: float32 [768, 768], P('dp'), may hold values from -1.75 to 1.75
- expand_average: float32 [768, 3072], P('dp'), may hold values from -0.21875 to 0.21875
- reduce_average: float32 [3072, 768], P('dp'), may hold values from -0.109375 to 0.109375
- gains_average: float32 [2, 768], P(None, 'dp'), may hold values from 0.5 to 1.5
- bias_average: float32 [7680], P('dp'), may hold values from -1.5 to 1.5
Outputs:
- layer_out: bfloat16 [32768, 768], P('dp')
- grad_input: bfloat16 [32768, 768], P('dp')
- qkv_grad: float32 [768, 2304], P('dp')
- proj_grad: float32 [768, 768], P('dp')
- expand_grad: float32 [768, 3072], P('dp')
- reduce_grad: float32 [3072, 768], P('dp')
- gains_grad: float32 [2, 768], P(None, 'dp')
- bias_grad: float32 [7680], P('dp')
- qkv_master: float32 [768, 2304], P('dp')
- proj_master: float32 [768, 768], P('dp')
- expand_master: float32 [768, 3072], P('dp')
- reduce_master: float32 [3072, 768], P('dp')
- gains_master: float32 [2, 768], P(None, 'dp')
- bias_master: float32 [7680], P('dp')
- qkv_velocity: float32 [768, 2304], P('dp')
- proj_velocity: float32 [768, 768], P('dp')
- expand_velocity: float32 [768, 3072], P('dp')
- reduce_velocity: float32 [3072, 768], P('dp')
- gains_velocity: float32 [2, 768], P(None, 'dp')
- bias_velocity: float32 [7680], P('dp')
- qkv_smooth: float32 [768, 2304], P('dp')
- proj_smooth: float32 [768, 768], P('dp')
- expand_smooth: float32 [768, 3072], P('dp')
- reduce_smooth: float32 [3072, 768], P('dp')
- gains_smooth: float32 [2, 768], P(None, 'dp')
- bias_smooth: float32 [7680], P('dp')
Inputs may be any that keep to these rules, and one draw needn't show every extreme that they name: `segment_ids`: each row lists one device's utterances: numbers 0 to 3 in order, each a run of 1 to 512 frames, one of exactly 512. `frame_valid`: 1 marks a frame with audio.
All inputs are finite; a program needn't handle non-finite values. No bound on the sum of `frame_valid` on one device may be relied on, other than what follows from the above.
Results may differ from a plain program's by a relative error of at most 0.015.
The roundings to bfloat16 on the way count: a program that leaves them out, or rounds other values in their place, can miss the bound.
Values may be sent and summed in bfloat16 or wider, within the bound.
A program may use at most 320 MiB of HBM per device.

v0:
```python
import math
import jax
import jax.numpy as jnp
from jax import lax
from jax.sharding import PartitionSpec as P

D = 768
H = 12
HD = 64
FF = 3072
EPSILON = 1e-05
MASKED = -1000000000.0
rate_matrix = 0.04
rate_proj = 0.5
rate_small = 0.2


def layer_norm(residual, gain_row, offset):
    center = residual - jnp.mean(residual, axis=-1, keepdims=True)
    spread = jnp.mean(center * center, axis=-1, keepdims=True)
    return center * lax.rsqrt(spread + EPSILON) * gain_row + offset


def gelu_exact(argument):
    return 0.5 * argument * (1.0 + jax.scipy.special.erf(argument * 0.7071067811865476))


def masked_scores(queries, key_heads, segments, present, first_row, block_rows):
    query_part = queries[first_row : first_row + block_rows]
    scores = (
        jnp.einsum("qhe,khe->hqk", query_part, key_heads, preferred_element_type=jnp.float32)
        * 0.125
    )
    column = jnp.arange(key_heads.shape[0])
    row_ids = column[first_row : first_row + block_rows]
    allowed = (segments[first_row : first_row + block_rows, None] == segments[None, :]) & (
        (present[None, :] > 0) | (row_ids[:, None] == column[None, :])
    )
    return (jnp.where(allowed[None], scores, MASKED), query_part)


def nesterov(master, gradient, moment, average, step_rate):
    velocity = 0.5 * moment + gradient
    renewed = master - step_rate * (gradient + 0.5 * velocity)
    smooth = 0.5 * average + 0.5 * renewed
    return (renewed, velocity, smooth)


def local(
    features,
    pos_conv,
    segment_ids,
    frame_valid,
    cotangent,
    qkv_weight,
    proj_weight,
    expand_weight,
    reduce_weight,
    norm_gains,
    bias_vector,
    qkv_moment,
    proj_moment,
    expand_moment,
    reduce_moment,
    gains_moment,
    bias_moment,
    qkv_average,
    proj_average,
    expand_average,
    reduce_average,
    gains_average,
    bias_average,
):
    row_count = features.shape[0]
    block_rows = min(512, row_count)
    segments = segment_ids[0]
    present = frame_valid[0]
    valid_col = present.astype(jnp.float32)[:, None]
    qkv_full, proj_full, expand_full, reduce_full, gains_low, bias_low = (
        lax.all_gather(qkv_weight.astype(jnp.bfloat16), "dp", axis=0, tiled=True),
        lax.all_gather(proj_weight.astype(jnp.bfloat16), "dp", axis=0, tiled=True),
        lax.all_gather(expand_weight.astype(jnp.bfloat16), "dp", axis=0, tiled=True),
        lax.all_gather(reduce_weight.astype(jnp.bfloat16), "dp", axis=0, tiled=True),
        lax.all_gather(norm_gains.astype(jnp.bfloat16), "dp", axis=1, tiled=True),
        lax.all_gather(bias_vector.astype(jnp.bfloat16), "dp", axis=0, tiled=True),
    )
    gains_full = gains_low.astype(jnp.float32)
    bias_full = bias_low.astype(jnp.float32)
    bias_query = bias_full[0:D]
    bias_value = bias_full[D : 2 * D]
    bias_proj = bias_full[2 * D : 3 * D]
    bias_expand = bias_full[3 * D : 3 * D + FF]
    bias_reduce = bias_full[3 * D + FF : 4 * D + FF]
    offset_first = bias_full[4 * D + FF : 5 * D + FF]
    offset_second = bias_full[5 * D + FF : 6 * D + FF]
    entry_sum = (features.astype(jnp.float32) + pos_conv.astype(jnp.float32)) * valid_col
    entry_low = entry_sum.astype(jnp.bfloat16)
    qkv_bias = jnp.concatenate([bias_query, jnp.zeros((D,), jnp.float32), bias_value])
    qkv_rows = (jnp.dot(entry_low, qkv_full, preferred_element_type=jnp.float32) + qkv_bias).astype(
        jnp.bfloat16
    )
    shaped = qkv_rows.reshape(row_count, 3, H, HD)
    queries = shaped[:, 0]
    key_heads = shaped[:, 1]
    values = shaped[:, 2]
    pieces = []
    log_totals = []
    for first_row in range(0, row_count, block_rows):
        scores, query_part = masked_scores(
            queries, key_heads, segments, present, first_row, block_rows
        )
        maximum = jnp.max(scores, axis=-1, keepdims=True)
        exponent = jnp.exp(scores - maximum)
        row_total = jnp.sum(exponent, axis=-1, keepdims=True)
        weights_now = (exponent / row_total).astype(jnp.bfloat16)
        pieces.append(
            jnp.einsum("hqk,khe->qhe", weights_now, values, preferred_element_type=jnp.float32)
        )
        log_totals.append(maximum + jnp.log(row_total))
    context = jnp.concatenate(pieces, axis=0).reshape(row_count, D).astype(jnp.bfloat16)
    attended = jnp.dot(context, proj_full, preferred_element_type=jnp.float32) + bias_proj
    normed, first_norm_back = jax.vjp(layer_norm, entry_sum + attended, gains_full[0], offset_first)
    normed_low = normed.astype(jnp.bfloat16)
    pre_act = jnp.dot(normed_low, expand_full, preferred_element_type=jnp.float32) + bias_expand
    activated, gelu_back = jax.vjp(gelu_exact, pre_act)
    act_low = activated.astype(jnp.bfloat16)
    ffn_out = jnp.dot(act_low, reduce_full, preferred_element_type=jnp.float32) + bias_reduce
    layer_float, second_norm_back = jax.vjp(
        layer_norm, normed + ffn_out, gains_full[1], offset_second
    )
    layer_out = layer_float.astype(jnp.bfloat16)
    qkv_back, proj_back, expand_back, reduce_back = (
        lax.all_gather(qkv_weight.astype(jnp.bfloat16), "dp", axis=0, tiled=True),
        lax.all_gather(proj_weight.astype(jnp.bfloat16), "dp", axis=0, tiled=True),
        lax.all_gather(expand_weight.astype(jnp.bfloat16), "dp", axis=0, tiled=True),
        lax.all_gather(reduce_weight.astype(jnp.bfloat16), "dp", axis=0, tiled=True),
    )
    grad_second, grad_gain_two, grad_offset_two = second_norm_back(cotangent.astype(jnp.float32))
    grad_ffn = grad_second.astype(jnp.bfloat16)
    grad_bias_reduce = jnp.sum(grad_ffn, axis=0, dtype=jnp.float32)
    grad_reduce = jnp.einsum("tf,td->fd", act_low, grad_ffn, preferred_element_type=jnp.float32)
    grad_hidden = jnp.einsum("td,fd->tf", grad_ffn, reduce_back, preferred_element_type=jnp.float32)
    (grad_pre_float,) = gelu_back(grad_hidden)
    grad_pre = grad_pre_float.astype(jnp.bfloat16)
    grad_bias_expand = jnp.sum(grad_pre, axis=0, dtype=jnp.float32)
    grad_expand = jnp.einsum("td,tf->df", normed_low, grad_pre, preferred_element_type=jnp.float32)
    grad_normed = grad_second + jnp.einsum(
        "tf,df->td", grad_pre, expand_back, preferred_element_type=jnp.float32
    )
    grad_first, grad_gain_one, grad_offset_one = first_norm_back(grad_normed)
    grad_branch = grad_first.astype(jnp.bfloat16)
    grad_bias_proj = jnp.sum(grad_branch, axis=0, dtype=jnp.float32)
    grad_proj = jnp.einsum("td,te->de", context, grad_branch, preferred_element_type=jnp.float32)
    grad_context = jnp.einsum(
        "te,de->td", grad_branch, proj_back, preferred_element_type=jnp.float32
    )
    grad_context = grad_context.astype(jnp.bfloat16).reshape(row_count, H, HD)
    query_grads = []
    key_grad = jnp.zeros((row_count, H, HD), jnp.float32)
    value_grad = jnp.zeros((row_count, H, HD), jnp.float32)
    for block_index, first_row in enumerate(range(0, row_count, block_rows)):
        scores, query_part = masked_scores(
            queries, key_heads, segments, present, first_row, block_rows
        )
        prob_block = jnp.exp(scores - log_totals[block_index])
        context_part = grad_context[first_row : first_row + block_rows]
        prob_grad = jnp.einsum(
            "qhe,khe->hqk", context_part, values, preferred_element_type=jnp.float32
        )
        row_dot = jnp.sum(prob_block * prob_grad, axis=-1, keepdims=True)
        score_grad = (prob_block * (prob_grad - row_dot)).astype(jnp.bfloat16)
        query_grads.append(
            0.125
            * jnp.einsum("hqk,khe->qhe", score_grad, key_heads, preferred_element_type=jnp.float32)
        )
        key_grad = key_grad + 0.125 * jnp.einsum(
            "hqk,qhe->khe", score_grad, query_part, preferred_element_type=jnp.float32
        )
        value_grad = value_grad + jnp.einsum(
            "hqk,qhe->khe",
            prob_block.astype(jnp.bfloat16),
            context_part,
            preferred_element_type=jnp.float32,
        )
    grad_qkv_low = jnp.stack([jnp.concatenate(query_grads, axis=0), key_grad, value_grad], axis=1)
    grad_qkv_low = grad_qkv_low.reshape(row_count, 3 * D).astype(jnp.bfloat16)
    grad_bias_query = jnp.sum(grad_qkv_low[:, 0:D], axis=0, dtype=jnp.float32)
    grad_bias_value = jnp.sum(grad_qkv_low[:, 2 * D : 3 * D], axis=0, dtype=jnp.float32)
    grad_qkv = jnp.einsum("td,te->de", entry_low, grad_qkv_low, preferred_element_type=jnp.float32)
    grad_entry = grad_first + jnp.einsum(
        "te,de->td", grad_qkv_low, qkv_back, preferred_element_type=jnp.float32
    )
    grad_input = (grad_entry * valid_col).astype(jnp.bfloat16)
    grad_gains = jnp.stack([grad_gain_one, grad_gain_two], axis=0)
    grad_bias = jnp.concatenate(
        [
            grad_bias_query,
            grad_bias_value,
            grad_bias_proj,
            grad_bias_expand,
            grad_bias_reduce,
            grad_offset_one,
            grad_offset_two,
        ]
    )
    qkv_grad, proj_grad, expand_grad, reduce_grad, gains_grad, bias_grad = (
        lax.psum_scatter(grad_qkv, "dp", scatter_dimension=0, tiled=True),
        lax.psum_scatter(grad_proj, "dp", scatter_dimension=0, tiled=True),
        lax.psum_scatter(grad_expand, "dp", scatter_dimension=0, tiled=True),
        lax.psum_scatter(grad_reduce, "dp", scatter_dimension=0, tiled=True),
        lax.psum_scatter(grad_gains, "dp", scatter_dimension=1, tiled=True),
        lax.psum_scatter(grad_bias, "dp", scatter_dimension=0, tiled=True),
    )
    frame_total = lax.axis_size("dp") * row_count
    matrix_rate = rate_matrix / math.sqrt(frame_total)
    proj_step = rate_proj / math.sqrt(frame_total)
    small_step = rate_small / math.sqrt(frame_total)
    qkv_new = nesterov(qkv_weight, qkv_grad, qkv_moment, qkv_average, matrix_rate)
    proj_new = nesterov(proj_weight, proj_grad, proj_moment, proj_average, proj_step)
    expand_new = nesterov(expand_weight, expand_grad, expand_moment, expand_average, matrix_rate)
    reduce_new = nesterov(reduce_weight, reduce_grad, reduce_moment, reduce_average, matrix_rate)
    gains_new = nesterov(norm_gains, gains_grad, gains_moment, gains_average, small_step)
    bias_new = nesterov(bias_vector, bias_grad, bias_moment, bias_average, small_step)
    return (
        layer_out,
        grad_input,
        qkv_grad,
        proj_grad,
        expand_grad,
        reduce_grad,
        gains_grad,
        bias_grad,
        qkv_new[0],
        proj_new[0],
        expand_new[0],
        reduce_new[0],
        gains_new[0],
        bias_new[0],
        qkv_new[1],
        proj_new[1],
        expand_new[1],
        reduce_new[1],
        gains_new[1],
        bias_new[1],
        qkv_new[2],
        proj_new[2],
        expand_new[2],
        reduce_new[2],
        gains_new[2],
        bias_new[2],
    )


def solution(mesh):
    in_specs = (
        P("dp", None),
        P("dp", None),
        P("dp", None),
        P("dp", None),
        P("dp", None),
        P("dp", None),
        P("dp", None),
        P("dp", None),
        P("dp", None),
        P(None, "dp"),
        P("dp"),
        P("dp", None),
        P("dp", None),
        P("dp", None),
        P("dp", None),
        P(None, "dp"),
        P("dp"),
        P("dp", None),
        P("dp", None),
        P("dp", None),
        P("dp", None),
        P(None, "dp"),
        P("dp"),
    )
    out_specs = (
        P("dp", None),
        P("dp", None),
        P("dp", None),
        P("dp", None),
        P("dp", None),
        P("dp", None),
        P(None, "dp"),
        P("dp"),
        P("dp", None),
        P("dp", None),
        P("dp", None),
        P("dp", None),
        P(None, "dp"),
        P("dp"),
        P("dp", None),
        P("dp", None),
        P("dp", None),
        P("dp", None),
        P(None, "dp"),
        P("dp"),
        P("dp", None),
        P("dp", None),
        P("dp", None),
        P("dp", None),
        P(None, "dp"),
        P("dp"),
    )
    return jax.shard_map(local, mesh=mesh, in_specs=in_specs, out_specs=out_specs, check_vma=False)
```

profile of v0, /device:TPU:0, one launch (start us, length us, event | category | flops | bytes accessed | tf_op | source)
XLA Modules:
  0.0 941.1 jit_solution(3668679954728577496)
XLA Ops:
  7.3 1.7 convert_element_type.123
  9.1 1.5 convert_element_type.130
  10.7 1.6 convert_element_type.134
  12.4 1.6 convert_element_type.136
  14.1 0.7 compare_reduce_fusion
  16.4 42.3 %all-reduce = bf16[7680]{0:T(1024)(128)(2,1)S(1)} all-reduce(bf16[7680]{0:T(1024)(128)(2,1)S(1)} %dynamic-update-slice), channel_id=1, replica_groups=mesh['dp'=32] {'dp'}, use_global_device_ids=true, to_apply=%add | all-reduce | flops 7680 | bytes 30720
  61.3 40.0 %all-gather = bf16[32,24,2]{1,2,0:T(2,128)(2,1)S(1)} all-gather(bf16[1,24,2]{1,2,0:T(2,128)(2,1)S(1)} %convert_bitcast_fusion), channel_id=1, replica_groups=mesh['dp'=32] {'dp'}, dimensions={0}, use_global_device_ids=true | all-gather | bytes 3168 | tf_op jit(solution)/shard_map/all_gather | solution.py:84
  102.1 1.6 copy.83
  103.8 1.7 copy.78
  105.5 1.6 copy.79
  107.1 2.0 fusion.21
  109.1 9.3 add_convert_fusion.1
  118.4 6.7 copy.80
  125.1 14.5 %fusion.13 = (f32[12,512]{1,0:T(8,128)S(1)}, f32[12,512,1024]{2,1,0:T(8,128)}) fusion(pred[512,1024]{1,0:T(8,128)(4,1)} %get-tuple-element.180, bf16[1024,3,12,64]{0,3,2,1:T(8,128)(2,1)} %bitcast.96), kind=kOutput, calls=%fused_computation.28 | convolution fusion | flops 824174592 | bytes 28073984 | tf_op jit(solution)/shard_map/qhe,khe->hqk/dot_general | solution.py:31
  139.6 12.4 %fusion.1 = f32[12,512]{1,0:T(8,128)S(1)} fusion(f32[12,512]{1,0:T(8,128)S(1)} %get-tuple-element.185, f32[12,512,1024]{2,1,0:T(8,128)} %get-tuple-element.186, pred[512,1024]{1,0:T(8,128)(4,1)} %get-tuple-element.180), kind=kLoop, calls=%fused_computation.13 | loop fusion | flops 25159680 | bytes 25739264 | tf_op jit(solution)/shard_map/reduce_sum | solution.py:114
  152.0 3.6 copy-done.1
  155.6 10.1 %fusion.35 = bf16[512,12,64]{0,2,1:T(8,128)(2,1)} fusion(f32[12,512]{1,0:T(8,128)S(1)} %fusion.1, f32[12,512]{1,0:T(8,128)S(1)} %get-tuple-element.185, f32[12,512,1024]{2,1,0:T(8,128)S(1)} %copy-done.1, pred[512,1024]{1,0:T(8,128)(4,1)} %get-tuple-element.180, bf16[1024,3,12,64]{0,3,2,1:T(8,128)(2,1)S(1)} %bitcast.101), kind=kOutput, calls=%fused_computation.80 | convolution fusion | flops 837156864 | bytes 28114944 | tf_op jit(solution)/shard_map/hqk,khe->qhe/dot_general | solution.py:117
  165.7 10.9 %fusion.12 = (f32[12,512]{1,0:T(8,128)S(1)}, f32[12,512,1024]{2,1,0:T(8,128)}) fusion(pred[512,1024]{1,0:T(8,128)(4,1)S(1)} %get-tuple-element.179, bf16[1024,3,12,64]{0,3,2,1:T(8,128)(2,1)S(1)} %bitcast.102), kind=kOutput, calls=%fused_computation.27 | convolution fusion | flops 824174592 | bytes 28073984 | tf_op jit(solution)/shard_map/qhe,khe->hqk/dot_general | solution.py:31
  176.6 13.5 %fusion = f32[12,512]{1,0:T(8,128)} fusion(f32[12,512]{1,0:T(8,128)S(1)} %get-tuple-element.187, f32[12,512,1024]{2,1,0:T(8,128)} %get-tuple-element.188, pred[512,1024]{1,0:T(8,128)(4,1)S(1)} %get-tuple-element.179), kind=kLoop, calls=%fused_computation.12 | loop fusion | flops 25159680 | bytes 25739264 | tf_op jit(solution)/shard_map/reduce_sum | solution.py:114
  190.1 2.7 copy-done
  192.8 9.7 %fusion.34 = bf16[512,12,64]{0,2,1:T(8,128)(2,1)} fusion(f32[12,512]{1,0:T(8,128)} %fusion, f32[12,512]{1,0:T(8,128)S(1)} %get-tuple-element.187, f32[12,512,1024]{2,1,0:T(8,128)S(1)} %copy-done, pred[512,1024]{1,0:T(8,128)(4,1)S(1)} %get-tuple-element.179, bf16[1024,3,12,64]{0,3,2,1:T(8,128)(2,1)S(1)} %bitcast.103), kind=kOutput, calls=%fused_computation.79 | convolution fusion | flops 837156864 | bytes 28106752 | tf_op jit(solution)/shard_map/hqk,khe->qhe/dot_general | solution.py:117
  202.5 2.7 pad_maximum_fusion.1
  205.2 4.6 fusion.63
  210.7 12.9 %multiply_convert_fusion.2 = (bf16[1024,3072]{1,0:T(8,128)(2,1)}, f32[1024,3072]{1,0:T(8,128)}) fusion(f32[3072]{0:T(1024)S(1)} %copy-done.47, bf16[768,3072]{1,0:T(8,128)(2,1)} %all-gather.10.cloned.1.call-done, f32[1024,768]{0,1:T(8,128)S(1)} %get-tuple-element.190, f32[768]{0:T(1024)S(1)} %copy-done.48, f32[768]{0:T(1024)S(1)} %copy-done.39, ...), kind=kOutput, calls=%fused_computation.22 | convolution fusion | flops 4854644736 | bytes 26765312 | tf_op jit(solution)/shard_map/dot_general | solution.py:124
  223.6 39.0 %all-gather.12.cloned.1.call-done = bf16[3072,768]{1,0:T(8,128)(2,1)} async-done(((bf16[96,768]{1,0:T(8,128)(2,1)}), bf16[3072,768]{1,0:T(8,128)(2,1)}) %all-gather.12.cloned.1.call-update) | async-done | bytes 4718608 | tf_op jit(solution)/shard_map/all_gather | solution.py:83
  262.6 9.1 fusion.64
  271.7 1.7 fusion.16
  273.4 2.2 fusion.17
  275.6 3.5 convert_reduce_fusion.2
  279.2 15.4 %convert_reduce_fusion = (f32[3072]{0:T(1024)}, bf16[1024,3072]{1,0:T(8,128)(2,1)S(1)}) fusion(bf16[1024,768]{0,1:T(8,128)(2,1)S(1)} %get-tuple-element.165, bf16[3072,768]{1,0:T(8,128)(2,1)S(1)} %bitcast.128, f32[1024,3072]{1,0:T(8,128)} %get-tuple-element.192, f32[3072]{0:T(1024)S(1)} %copy-done.47), kind=kOutput, calls=%fused_computation.18 | convolution fusion | flops 4882166784 | bytes 25190400 | tf_op jit(solution)/shard_map/td,fd->tf/dot_general | solution.py:142
  294.6 7.1 multiply_reduce_fusion.2
  301.7 0.8 fusion.59
  302.5 1.6 copy-done.12
  304.2 0.9 convert_reduce_fusion.3
  305.1 2.8 fusion.65
  307.9 1.4 convolution_convert_fusion
  309.4 1.0 copy-done.8
  310.4 13.6 %fusion.4 = f32[12,64,1024]{2,1,0:T(8,128)} fusion(bf16[512,12,64]{0,2,1:T(8,128)(2,1)S(1)} %bitcast.113, f32[12,512]{1,0:T(8,128)S(1)} %log_add_fusion, f32[12,512,1024]{2,1,0:T(8,128)} %get-tuple-element.186, pred[512,1024]{1,0:T(8,128)(4,1)S(1)} %copy-done.8), kind=kOutput, calls=%fused_computation.16 | convolution fusion | flops 830472192 | bytes 29646848 | tf_op jit(solution)/shard_map/hqk,qhe->khe/dot_general | solution.py:179
  324.0 20.3 %multiply_reduce_fusion = (f32[12,512]{1,0:T(8,128)S(1)}, f32[12,512,1024]{2,1,0:T(8,128)}) fusion(f32[12,512]{1,0:T(8,128)S(1)} %log_add_fusion, f32[12,512,1024]{2,1,0:T(8,128)} %get-tuple-element.186, pred[512,1024]{1,0:T(8,128)(4,1)S(1)} %copy-done.8, bf16[512,12,64]{0,2,1:T(8,128)(2,1)S(1)} %bitcast.114, bf16[1024,3,12,64]{0,3,2,1:T(8,128)(2,1)} %bitcast.97), kind=kOutput, calls=%fused_computation.1 | convolution fusion | flops 836757504 | bytes 53264384 | tf_op jit(solution)/shard_map/qhe,khe->hqk/dot_general | solution.py:167
  344.2 20.3 %multiply_reduce_fusion.1 = (f32[12,512]{1,0:T(8,128)S(1)}, f32[12,512,1024]{2,1,0:T(8,128)}) fusion(f32[12,512]{1,0:T(8,128)S(1)} %log_add_fusion.1, f32[12,512,1024]{2,1,0:T(8,128)} %get-tuple-element.188, pred[512,1024]{1,0:T(8,128)(4,1)S(1)} %copy-done.6, bf16[512,12,64]{0,2,1:T(8,128)(2,1)S(1)} %bitcast.111, bf16[1024,3,12,64]{0,3,2,1:T(8,128)(2,1)} %bitcast.98), kind=kOutput, calls=%fused_computation.4 | convolution fusion | flops 836757504 | bytes 53264384 | tf_op jit(solution)/shard_map/qhe,khe->hqk/dot_general | solution.py:167
  364.6 42.7 %multiply_convert_fusion = (bf16[12,512,1024]{2,1,0:T(8,128)(2,1)}, bf16[12,512,1024]{2,1,0:T(8,128)(2,1)}) fusion(f32[12,512,1024]{2,1,0:T(8,128)} %get-tuple-element.199, f32[12,512]{1,0:T(8,128)S(1)} %get-tuple-element.198, f32[12,512]{1,0:T(8,128)S(1)} %log_add_fusion, f32[12,512,1024]{2,1,0:T(8,128)} %get-tuple-element.186, ...), kind=kLoop, calls=%fused_computation | loop fusion | flops 75497472 | bytes 126976000 | tf_op jit(solution)/shard_map/convert_element_type | solution.py:171
  407.3 9.5 %fusion.32 = bf16[512,12,64]{0,2,1:T(8,128)(2,1)} fusion(bf16[12,512,1024]{2,1,0:T(8,128)(2,1)} %get-tuple-element.203, bf16[1024,3,12,64]{0,3,2,1:T(8,128)(2,1)S(1)} %bitcast.106), kind=kOutput, calls=%fused_computation.77 | convolution fusion | flops 806092800 | bytes 14942208 | tf_op jit(solution)/shard_map/hqk,khe->qhe/dot_general | solution.py:174
  416.8 8.6 fusion.40
  425.5 9.2 fusion.33
  434.7 7.5 fusion.29
  442.5 12.4 %fusion.26 = bf16[1024,1,12,64]{0,3,2,1:T(8,128)(2,1)S(1)} fusion(f32[12,64,1024]{2,1,0:T(8,128)S(1)} %copy-done.62, bf16[512,12,64]{0,2,1:T(8,128)(2,1)S(1)} %bitcast.112, f32[12,512]{1,0:T(8,128)S(1)} %log_add_fusion.1, f32[12,512,1024]{2,1,0:T(8,128)} %get-tuple-element.188, pred[512,1024]{1,0:T(8,128)(4,1)S(1)} %copy-done.7), kind=kOutput, calls=%fused_computation.73 | convolution fusion | flops 832045056 | bytes 31219712 | tf_op jit(solution)/shard_map/hqk,qhe->khe/dot_general | solution.py:179
  455.5 2.2 copy-done.9
  457.8 6.0 fusion.41
  463.8 1.8 copy-done.11
  465.6 10.5 %fusion.54 = f32[768,3072]{1,0:T(8,128)} fusion(bf16[1024,3072]{1,0:T(8,128)(2,1)} %copy-done.63, f32[1024,768]{0,1:T(8,128)S(1)} %copy-done.11, f32[768]{0:T(1024)S(1)} %copy-done.49, f32[768]{0:T(1024)S(1)} %copy-done.39, f32[1024]{0:T(1024)S(1)} %fusion.44, f32[1024]{0:T(1024)S(1)} %broadcast_multiply_fusion.1), kind=kOutput, calls=%fused_computation.141 | convolution fusion | flops 4835770368 | bytes 18888704 | tf_op jit(solution)/shard_map/td,tf->df/dot_general | solution.py:146
  476.2 1.3 copy-done.24
  477.5 10.5 %fusion.66 = f32[3072,768]{1,0:T(8,128)} fusion(bf16[1024,3072]{1,0:T(8,128)(2,1)} %get-tuple-element.191, bf16[1024,768]{0,1:T(8,128)(2,1)S(1)} %copy-done.24), kind=kOutput, calls=%fused_computation.151 | convolution fusion | flops 4831838208 | bytes 17301504 | tf_op jit(solution)/shard_map/tf,td->fd/dot_general | solution.py:141
  488.8 2.8 copy.86
  491.6 8.5 multiply_convert_fusion.3
  500.3 2.8 copy.87
  503.1 2.5 convert_reduce_fusion.4
  505.8 40.1 %all-reduce.3 = (f32[2,768]{1,0:T(2,128)S(1)}, f32[7680]{0:T(1024)S(1)}) all-reduce(f32[2,768]{1,0:T(2,128)S(1)} %pad_maximum_fusion.3, f32[7680]{0:T(1024)S(1)} %constant_dynamic-update-slice_fusion), channel_id=6, replica_groups=mesh['dp'=32] {'dp'}, use_global_device_ids=true, to_apply=%region_20.21.clone | all-reduce | flops 9216 | bytes 73728
  547.3 1.6 add_multiply_fusion.4
  548.9 99.7 %reduce-scatter.6.cloned.1.call-done = f32[24,2304]{1,0:T(8,128)} async-done(((f32[768,2304]{1,0:T(8,128)}), f32[24,2304]{1,0:T(8,128)}) %reduce-scatter.6.cloned.1.call-update) | async-done | bytes 221200 | tf_op jit(solution)/shard_map/reduce_scatter | solution.py:207
  648.6 1.8 add_multiply_fusion.3
  650.4 139.4 %reduce-scatter.10.cloned.1.call-done = f32[24,3072]{1,0:T(8,128)} async-done(((f32[768,3072]{1,0:T(8,128)}), f32[24,3072]{1,0:T(8,128)}) %reduce-scatter.10.cloned.1.call-update) | async-done | bytes 294928 | tf_op jit(solution)/shard_map/reduce_scatter | solution.py:209
  789.8 1.9 add_multiply_fusion.2
  791.8 140.1 %reduce-scatter.12.cloned.1.call-done = f32[96,768]{1,0:T(8,128)} async-done(((f32[3072,768]{1,0:T(8,128)}), f32[96,768]{1,0:T(8,128)}) %reduce-scatter.12.cloned.1.call-update) | async-done | bytes 294928 | tf_op jit(solution)/shard_map/reduce_scatter | solution.py:210
  931.9 1.9 add_multiply_fusion.1
  (200 shorter events, 9.5 us)
Async XLA Ops:
  7.2 94.9 %copy-start.17 = (bf16[1024,768]{1,0:T(8,128)(2,1)S(1)}, bf16[1024,768]{1,0:T(8,128)(2,1)}, u32[]{:S(2)}) copy-start(bf16[1024,768]{1,0:T(8,128)(2,1)} %param.27) | copy-start | bytes 4718596
  7.2 96.6 %copy-start.18 = (bf16[1024,768]{1,0:T(8,128)(2,1)S(1)}, bf16[1024,768]{1,0:T(8,128)(2,1)}, u32[]{:S(2)}) copy-start(bf16[1024,768]{1,0:T(8,128)(2,1)} %param.23) | copy-start | bytes 4718596
  7.2 101.9 %all-gather.6.cloned.1.call-start = ((), (), s32[]{:S(2)}) async-start(), calls=%async_computation.4 | async-start | bytes 3649536 | tf_op jit(solution)/shard_map/all_gather | solution.py:80
  9.0 196.1 %all-gather.8.cloned.1.call-start = ((), (), s32[]{:S(2)}) async-start(), calls=%async_computation.5 | async-start | bytes 1216512 | tf_op jit(solution)/shard_map/all_gather | solution.py:81
  10.6 200.0 %all-gather.10.cloned.1.call-start = ((), (), s32[]{:S(2)}) async-start(), calls=%async_computation.6 | async-start | bytes 4866048 | tf_op jit(solution)/shard_map/all_gather | solution.py:82
  12.3 250.3 %all-gather.12.cloned.1.call-start = ((), (), s32[]{:S(2)}) async-start(), calls=%async_computation.7 | async-start | bytes 4866048 | tf_op jit(solution)/shard_map/all_gather | solution.py:83
  14.1 533.3 %reduce-scatter.8.cloned.1.call-start = ((), (), s32[]{:S(2)}) async-start(), calls=%async_computation.9 | async-start | bytes 2433024 | tf_op jit(solution)/shard_map/reduce_scatter | solution.py:208
  15.5 189.7 %copy-start.52 = (f32[1,1024]{1,0:T(1,128)}, f32[1,1024]{1,0:T(1,128)S(1)}, u32[]{:S(2)}) copy-start(f32[1,1024]{1,0:T(1,128)S(1)} %convert_element_type.120) | copy-start | bytes 12292
  103.8 3.3 copy-start.42
  109.1 81.0 %copy-start.5 = (pred[512,1024]{1,0:T(8,128)(4,1)}, pred[512,1024]{1,0:T(8,128)(4,1)S(1)}, u32[]{:S(2)}) copy-start(pred[512,1024]{1,0:T(8,128)(4,1)S(1)} %get-tuple-element.179) | copy-start | bytes 1572868
  125.1 27.0 %copy-start.2 = (bf16[1024,2304]{0,1:T(8,128)(2,1)S(1)}, bf16[1024,2304]{0,1:T(8,128)(2,1)}, u32[]{:S(2)}) copy-start(bf16[1024,2304]{0,1:T(8,128)(2,1)} %copy.80) | copy-start | bytes 14155780
  139.6 16.0 %copy-start.1 = (f32[12,512,1024]{2,1,0:T(8,128)S(1)}, f32[12,512,1024]{2,1,0:T(8,128)}, u32[]{:S(2)}) copy-start(f32[12,512,1024]{2,1,0:T(8,128)} %get-tuple-element.186) | copy-start | bytes 75497472
  176.6 16.1 %copy-start = (f32[12,512,1024]{2,1,0:T(8,128)S(1)}, f32[12,512,1024]{2,1,0:T(8,128)}, u32[]{:S(2)}) copy-start(f32[12,512,1024]{2,1,0:T(8,128)} %get-tuple-element.188) | copy-start | bytes 75497472
  209.8 91.8 %copy-start.10 = (f32[1024,768]{0,1:T(8,128)}, f32[1024,768]{0,1:T(8,128)S(1)}, u32[]{:S(2)}) copy-start(f32[1024,768]{0,1:T(8,128)S(1)} %get-tuple-element.190) | copy-start | bytes 9437188
  210.7 51.9 %copy-start.50 = (f32[768]{0:T(1024)S(1)}, f32[768]{0:T(1024)}, u32[]{:S(2)}) copy-start(f32[768]{0:T(1024)} %get-tuple-element.174) | copy-start | bytes 9220
  262.6 9.1 copy-start.4
  262.6 9.1 copy-start.38
  271.7 7.5 slice-start.4
  273.4 5.8 slice-start.5
  275.6 19.0 %slice-start.2 = ((s8[4718592]{0:T(1024)(128)(4,1)}), s8[4194304]{0:T(1024)(128)(4,1)S(1)}, s32[]{:S(2)}) async-start(s8[4718592]{0:T(1024)(128)(4,1)} %bitcast.125), calls=%async_computation.14 | async-start | bytes 8388608
  279.2 15.4 %copy-start.23 = (bf16[1024,768]{0,1:T(8,128)(2,1)}, bf16[1024,768]{0,1:T(8,128)(2,1)S(1)}, u32[]{:S(2)}) copy-start(bf16[1024,768]{0,1:T(8,128)(2,1)S(1)} %get-tuple-element.165) | copy-start | bytes 4718596
  279.2 15.4 %slice-start.3 = ((s8[4718592]{0:T(1024)(128)(4,1)}), s8[524288]{0:T(1024)(128)(4,1)S(1)}, s32[]{:S(2)}) async-start(s8[4718592]{0:T(1024)(128)(4,1)} %bitcast.125), calls=%async_computation.15 | async-start | bytes 1048576
  294.6 7.1 copy-start.63
  302.5 2.6 copy-start.22
  305.1 2.8 copy-start.61
  309.4 34.8 %copy-start.15 = (bf16[512,768]{0,1:T(8,128)(2,1)}, bf16[512,768]{0,1:T(8,128)(2,1)S(1)}, u32[]{:S(2)}) copy-start(bf16[512,768]{0,1:T(8,128)(2,1)S(1)} %get-tuple-element.171) | copy-start | bytes 2359300
  324.0 20.3 %copy-start.6 = (pred[512,1024]{1,0:T(8,128)(4,1)S(1)}, pred[512,1024]{1,0:T(8,128)(4,1)}, u32[]{:S(2)}) copy-start(pred[512,1024]{1,0:T(8,128)(4,1)} %copy-done.5) | copy-start | bytes 1572868
  344.2 63.1 %slice-start = ((s8[4718592]{0:T(1024)(128)(4,1)}), s8[524288]{0:T(1024)(128)(4,1)S(1)}, s32[]{:S(2)}) async-start(s8[4718592]{0:T(1024)(128)(4,1)} %bitcast.104), calls=%async_computation.12 | async-start | bytes 1048576
  364.6 42.7 %slice-start.1 = ((s8[4718592]{0:T(1024)(128)(4,1)}), s8[4194304]{0:T(1024)(128)(4,1)S(1)}, s32[]{:S(2)}) async-start(s8[4718592]{0:T(1024)(128)(4,1)} %bitcast.104), calls=%async_computation.13 | async-start | bytes 8388608
  425.4 223.2 %reduce-scatter.6.cloned.1.call-start = ((), (), s32[]{:S(2)}) async-start(), calls=%async_computation.8 | async-start | bytes 7299072 | tf_op jit(solution)/shard_map/reduce_scatter | solution.py:207
  425.5 9.2 copy-start.3
  434.6 7.6 copy-start.14
  434.7 7.8 copy-start.7
  434.7 7.8 copy-start.16
  434.7 7.8 copy-start.62
  454.9 2.8 copy-start.20
  454.9 2.8 copy-start.21
  454.9 2.8 copy-start.53
  463.8 326.1 %reduce-scatter.10.cloned.1.call-start = ((), (), s32[]{:S(2)}) async-start(), calls=%async_computation.10 | async-start | bytes 9732096 | tf_op jit(solution)/shard_map/reduce_scatter | solution.py:209
  476.1 455.8 %reduce-scatter.12.cloned.1.call-start = ((), (), s32[]{:S(2)}) async-start(), calls=%async_computation.11 | async-start | bytes 9732096 | tf_op jit(solution)/shard_map/reduce_scatter | solution.py:210
  488.1 3.5 copy-start.13
  500.1 5.5 copy-start.44
  500.2 5.5 copy-start.46
  500.2 5.6 copy-start.43
  500.2 5.6 copy-start.54
  500.2 5.6 copy-start.45
  500.2 45.8 %copy-start.55 = (f32[2,24]{1,0:T(2,128)S(1)}, f32[2,24]{1,0:T(2,128)}, u32[]{:S(2)}) copy-start(f32[2,24]{1,0:T(2,128)} %param.32) | copy-start | bytes 580
  500.2 45.8 %copy-start.56 = (f32[2,24]{1,0:T(2,128)S(1)}, f32[2,24]{1,0:T(2,128)}, u32[]{:S(2)}) copy-start(f32[2,24]{1,0:T(2,128)} %param.44) | copy-start | bytes 580
  500.2 45.8 %copy-start.57 = (f32[2,24]{1,0:T(2,128)S(1)}, f32[2,24]{1,0:T(2,128)}, u32[]{:S(2)}) copy-start(f32[2,24]{1,0:T(2,128)} %param.38) | copy-start | bytes 580
  500.2 46.4 %copy-start.58 = (f32[240]{0:T(256)S(1)}, f32[240]{0:T(256)}, u32[]{:S(2)}) copy-start(f32[240]{0:T(256)} %param.33) | copy-start | bytes 2884
  500.2 46.4 %copy-start.59 = (f32[240]{0:T(256)S(1)}, f32[240]{0:T(256)}, u32[]{:S(2)}) copy-start(f32[240]{0:T(256)} %param.45) | copy-start | bytes 2884
  500.2 46.4 %copy-start.60 = (f32[240]{0:T(256)S(1)}, f32[240]{0:T(256)}, u32[]{:S(2)}) copy-start(f32[240]{0:T(256)} %param.39) | copy-start | bytes 2884
  500.2 47.1 %copy-start.28 = (f32[24,768]{1,0:T(8,128)S(1)}, f32[24,768]{1,0:T(8,128)}, u32[]{:S(2)}) copy-start(f32[24,768]{1,0:T(8,128)} %param.29) | copy-start | bytes 221188
  500.3 47.0 %copy-start.36 = (f32[24,768]{1,0:T(8,128)S(1)}, f32[24,768]{1,0:T(8,128)}, u32[]{:S(2)}) copy-start(f32[24,768]{1,0:T(8,128)} %param.41) | copy-start | bytes 221188
  500.3 47.0 %copy-start.37 = (f32[24,768]{1,0:T(8,128)S(1)}, f32[24,768]{1,0:T(8,128)}, u32[]{:S(2)}) copy-start(f32[24,768]{1,0:T(8,128)} %param.35) | copy-start | bytes 221188
  500.3 148.3 %copy-start.27 = (f32[24,2304]{1,0:T(8,128)S(1)}, f32[24,2304]{1,0:T(8,128)}, u32[]{:S(2)}) copy-start(f32[24,2304]{1,0:T(8,128)} %param.28) | copy-start | bytes 663556
  500.3 148.3 %copy-start.33 = (f32[24,2304]{1,0:T(8,128)S(1)}, f32[24,2304]{1,0:T(8,128)}, u32[]{:S(2)}) copy-start(f32[24,2304]{1,0:T(8,128)} %param.40) | copy-start | bytes 663556
  500.3 148.3 %copy-start.34 = (f32[24,2304]{1,0:T(8,128)S(1)}, f32[24,2304]{1,0:T(8,128)}, u32[]{:S(2)}) copy-start(f32[24,2304]{1,0:T(8,128)} %param.34) | copy-start | bytes 663556
  503.1 286.7 %copy-start.25 = (f32[24,3072]{1,0:T(8,128)S(1)}, f32[24,3072]{1,0:T(8,128)}, u32[]{:S(2)}) copy-start(f32[24,3072]{1,0:T(8,128)} %param.30) | copy-start | bytes 884740
  503.1 286.7 %copy-start.29 = (f32[24,3072]{1,0:T(8,128)S(1)}, f32[24,3072]{1,0:T(8,128)}, u32[]{:S(2)}) copy-start(f32[24,3072]{1,0:T(8,128)} %param.42) | copy-start | bytes 884740
  503.1 286.7 %copy-start.30 = (f32[24,3072]{1,0:T(8,128)S(1)}, f32[24,3072]{1,0:T(8,128)}, u32[]{:S(2)}) copy-start(f32[24,3072]{1,0:T(8,128)} %param.36) | copy-start | bytes 884740
  503.1 428.8 %copy-start.26 = (f32[96,768]{1,0:T(8,128)S(1)}, f32[96,768]{1,0:T(8,128)}, u32[]{:S(2)}) copy-start(f32[96,768]{1,0:T(8,128)} %param.31) | copy-start | bytes 884740
  503.1 428.8 %copy-start.31 = (f32[96,768]{1,0:T(8,128)S(1)}, f32[96,768]{1,0:T(8,128)}, u32[]{:S(2)}) copy-start(f32[96,768]{1,0:T(8,128)} %param.43) | copy-start | bytes 884740
  503.1 428.8 %copy-start.32 = (f32[96,768]{1,0:T(8,128)S(1)}, f32[96,768]{1,0:T(8,128)}, u32[]{:S(2)}) copy-start(f32[96,768]{1,0:T(8,128)} %param.37) | copy-start | bytes 884740
  (14 other events, 18.8 us)
Sparse Core Ops, SparseCore 0:
  11.5 62.8 all-gather.5
  77.9 52.8 all-gather.7
  134.2 62.5 all-gather.9
  200.2 62.3 all-gather.11
  425.5 97.9 reduce-scatter.7
  530.5 117.9 reduce-scatter.5
  655.1 134.7 reduce-scatter.9
  797.3 134.5 reduce-scatter.11
where the time goes:
time: 952 us; the launch traced here: 941 us
  waiting for transfers between devices  418 us (44%)
  matrix products  245 us (26%)
  blocking collectives  122 us (13%)
  other arithmetic  104 us (11%)
  local copies, waits for them, and re-layouts  35.9 us (4%)
  between operations  15.4 us (2%)
    reduce_scatter x1, waiting for transfers between devices, local(): lax.psum_scatter(grad_reduce, 'dp', scatter_dimension=0, tiled=True)  140 us
    reduce_scatter x1, waiting for transfers between devices, local(): lax.psum_scatter(grad_expand, 'dp', scatter_dimension=0, tiled=True)  139 us
    reduce_scatter x1, waiting for transfers between devices, local(): lax.psum_scatter(grad_qkv, 'dp', scatter_dimension=0, tiled=True)  99.7 us
    unnamed x2, blocking collectives  82.4 us
    convert_element_type x1, other arithmetic, local(): score_grad = (prob_block * (prob_grad - row_dot)).astype(jnp.bfloat16)  42.7 us
    dot_general x2, matrix products, local(): jnp.einsum('qhe,khe->hqk', context_part, values, preferred_element_type=j...  40.6 us
    all_gather x1, blocking collectives, local(): lax.all_gather(norm_gains.astype(jnp.bfloat16), 'dp', axis=1, tiled=True)  40 us
    all_gather x1, waiting for transfers between devices, local(): lax.all_gather(reduce_weight.astype(jnp.bfloat16), 'dp', axis=0, tiled=True)  39 us
  transfers between devices with their start and end apart: 8, of which 4 were waited for; matrix products, arithmetic and copies ran while one was open for 22% of the time, Pallas kernels for 0%

commit v1 on v0

--- a/solution.py
+++ b/solution.py
@@ -13,6 +13,18 @@
 rate_matrix = 0.04
 rate_proj = 0.5
 rate_small = 0.2
+
+
+def gather_by_bits(x, axis, dim):
+    ways, here, step = (lax.axis_size(axis), lax.axis_index(axis), x.shape[dim])
+    line, have = (x, 1)
+    while have < ways:
+        line = jnp.concatenate(
+            [line, lax.ppermute(line, axis, [(d, (d - have) % ways) for d in range(ways)])],
+            axis=dim,
+        )
+        have = 2 * have
+    return jnp.roll(line, here * step, axis=dim)
 
 
 def layer_norm(residual, gain_row, offset):
@@ -81,7 +93,7 @@
         lax.all_gather(proj_weight.astype(jnp.bfloat16), "dp", axis=0, tiled=True),
         lax.all_gather(expand_weight.astype(jnp.bfloat16), "dp", axis=0, tiled=True),
         lax.all_gather(reduce_weight.astype(jnp.bfloat16), "dp", axis=0, tiled=True),
-        lax.all_gather(norm_gains.astype(jnp.bfloat16), "dp", axis=1, tiled=True),
+        gather_by_bits(norm_gains.astype(jnp.bfloat16), "dp", 1),
         lax.all_gather(bias_vector.astype(jnp.bfloat16), "dp", axis=0, tiled=True),
     )
     gains_full = gains_low.astype(jnp.float32)

time: 952 us -> 945 us (level)
  blocking collectives: 122 us -> 80.6 us
  waiting for transfers between devices: 418 us -> 448 us
  starting transfers between devices: 0.33 us -> 11.7 us
    all_gather x1 -> x0, blocking collectives: 40 us -> none  [local(): lax.all_gather(norm_gains.astype(jnp.bfloat16), 'dp', axis=1, tiled=True)]
    all_gather x1, waiting for transfers between devices: 39 us -> 53 us  [local(): lax.all_gather(reduce_weight.astype(jnp.bfloat16), 'dp', axis=0, tiled=True)]
    ppermute x0 -> x5, starting transfers between devices: none -> 11.4 us  [gather_by_bits(): lax.ppermute(line, axis, [(d, (d - have) % ways) for d in range(ways)])]
    all_gather x1, waiting for transfers between devices: 0.02 us -> 11.4 us  [local(): lax.all_gather(expand_weight.astype(jnp.bfloat16), 'dp', axis=0, tiled=True)]
    unnamed x153 -> x147, local copies, waits for them, and re-layouts: 26.3 us -> 27.6 us
  transfers between devices with their start and end apart: 8 -> 13, of which waited for: 4 -> 7; matrix products, arithmetic and copies ran while one was open for 22% -> 22% of each run, Pallas kernels for 0% -> 0%
where the time goes in v1:
time: 945 us; the launch traced here: 941 us
  waiting for transfers between devices  448 us (47%)
  matrix products  244 us (26%)
  other arithmetic  104 us (11%)
  blocking collectives  80.6 us (9%)
  local copies, waits for them, and re-layouts  37.1 us (4%)
  between operations  15.2 us (2%)
  starting transfers between devices  11.7 us (1%)
    reduce_scatter x1, waiting for transfers between devices, local(): lax.psum_scatter(grad_reduce, 'dp', scatter_dimension=0, tiled=True)  140 us
    reduce_scatter x1, waiting for transfers between devices, local(): lax.psum_scatter(grad_expand, 'dp', scatter_dimension=0, tiled=True)  139 us
    reduce_scatter x1, waiting for transfers between devices, local(): lax.psum_scatter(grad_qkv, 'dp', scatter_dimension=0, tiled=True)  99.9 us
    unnamed x2, blocking collectives  80.6 us
    all_gather x1, waiting for transfers between devices, local(): lax.all_gather(reduce_weight.astype(jnp.bfloat16), 'dp', axis=0, tiled=True)  53 us
    convert_element_type x1, other arithmetic, local(): score_grad = (prob_block * (prob_grad - row_dot)).astype(jnp.bfloat16)  43 us
    dot_general x2, matrix products, local(): jnp.einsum('qhe,khe->hqk', context_part, values, preferred_element_type=j...  40.5 us
    unnamed x147, local copies, waits for them, and re-layouts  27.6 us
  transfers between devices with their start and end apart: 13, of which 7 were waited for; matrix products, arithmetic and copies ran while one was open for 22% of the time, Pallas kernels for 0%

profile of v1, /device:TPU:0, one launch (start us, length us, event | category | flops | bytes accessed | tf_op | source)
XLA Modules:
  0.0 941.2 jit_solution(9149370025845225686)
XLA Ops:
  7.3 1.7 convert_element_type.123
  9.0 1.5 convert_element_type.130
  10.6 1.6 convert_element_type.134
  13.0 6.4 collective-permute-start
  19.4 1.6 convert_element_type.136
  23.2 2.6 fusion.21
  26.7 2.8 collective-permute-done.1
  30.1 40.4 %all-reduce = bf16[7680]{0:T(1024)(128)(2,1)S(1)} all-reduce(bf16[7680]{0:T(1024)(128)(2,1)S(1)} %dynamic-update-slice), channel_id=1, replica_groups=mesh['dp'=32] {'dp'}, use_global_device_ids=true, to_apply=%add | all-reduce | flops 7680 | bytes 30720
  70.6 1.8 collective-permute-start.3
  74.4 2.1 collective-permute-start.4
  77.9 1.6 copy.71
  79.5 2.8 copy.68
  82.3 1.6 copy.69
  84.7 9.1 add_convert_fusion.1
  93.8 6.7 copy.70
  100.5 14.5 %fusion.13 = (f32[12,512]{1,0:T(8,128)S(1)}, f32[12,512,1024]{2,1,0:T(8,128)}) fusion(pred[512,1024]{1,0:T(8,128)(4,1)} %get-tuple-element.154, bf16[1024,3,12,64]{0,3,2,1:T(8,128)(2,1)} %bitcast.89), kind=kOutput, calls=%fused_computation.28 | convolution fusion | flops 824174592 | bytes 28073984 | tf_op jit(solution)/shard_map/qhe,khe->hqk/dot_general | solution.py:43
  115.1 12.3 %fusion.1 = f32[12,512]{1,0:T(8,128)S(1)} fusion(f32[12,512]{1,0:T(8,128)S(1)} %get-tuple-element.159, f32[12,512,1024]{2,1,0:T(8,128)} %get-tuple-element.160, pred[512,1024]{1,0:T(8,128)(4,1)} %get-tuple-element.154), kind=kLoop, calls=%fused_computation.13 | loop fusion | flops 25159680 | bytes 25739264 | tf_op jit(solution)/shard_map/reduce_sum | solution.py:126
  127.4 3.8 copy-done.1
  131.2 10.0 %fusion.35 = bf16[512,12,64]{0,2,1:T(8,128)(2,1)} fusion(f32[12,512]{1,0:T(8,128)S(1)} %fusion.1, f32[12,512]{1,0:T(8,128)S(1)} %get-tuple-element.159, f32[12,512,1024]{2,1,0:T(8,128)S(1)} %copy-done.1, pred[512,1024]{1,0:T(8,128)(4,1)} %get-tuple-element.154, bf16[1024,3,12,64]{0,3,2,1:T(8,128)(2,1)S(1)} %bitcast.94), kind=kOutput, calls=%fused_computation.80 | convolution fusion | flops 837156864 | bytes 28114944 | tf_op jit(solution)/shard_map/hqk,khe->qhe/dot_general | solution.py:129
  141.2 11.0 %fusion.12 = (f32[12,512]{1,0:T(8,128)S(1)}, f32[12,512,1024]{2,1,0:T(8,128)}) fusion(pred[512,1024]{1,0:T(8,128)(4,1)S(1)} %get-tuple-element.153, bf16[1024,3,12,64]{0,3,2,1:T(8,128)(2,1)S(1)} %bitcast.95), kind=kOutput, calls=%fused_computation.27 | convolution fusion | flops 824174592 | bytes 28073984 | tf_op jit(solution)/shard_map/qhe,khe->hqk/dot_general | solution.py:43
  152.1 12.9 %fusion = f32[12,512]{1,0:T(8,128)} fusion(f32[12,512]{1,0:T(8,128)S(1)} %get-tuple-element.161, f32[12,512,1024]{2,1,0:T(8,128)} %get-tuple-element.162, pred[512,1024]{1,0:T(8,128)(4,1)S(1)} %get-tuple-element.153), kind=kLoop, calls=%fused_computation.12 | loop fusion | flops 25159680 | bytes 25739264 | tf_op jit(solution)/shard_map/reduce_sum | solution.py:126
  165.1 2.7 copy-done
  167.7 9.9 %fusion.34 = bf16[512,12,64]{0,2,1:T(8,128)(2,1)} fusion(f32[12,512]{1,0:T(8,128)} %fusion, f32[12,512]{1,0:T(8,128)S(1)} %get-tuple-element.161, f32[12,512,1024]{2,1,0:T(8,128)S(1)} %copy-done, pred[512,1024]{1,0:T(8,128)(4,1)S(1)} %get-tuple-element.153, bf16[1024,3,12,64]{0,3,2,1:T(8,128)(2,1)S(1)} %bitcast.96), kind=kOutput, calls=%fused_computation.79 | convolution fusion | flops 837156864 | bytes 28106752 | tf_op jit(solution)/shard_map/hqk,khe->qhe/dot_general | solution.py:129
  177.7 2.7 pad_maximum_fusion.1
  180.4 4.6 fusion.63
  185.7 11.4 %all-gather.9.cloned.1.call-done = bf16[768,3072]{1,0:T(8,128)(2,1)} async-done(((bf16[24,3072]{1,0:T(8,128)(2,1)}), bf16[768,3072]{1,0:T(8,128)(2,1)}) %all-gather.9.cloned.1.call-update) | async-done | bytes 4718608 | tf_op jit(solution)/shard_map/all_gather | solution.py:94
  197.1 12.7 %multiply_convert_fusion.2 = (bf16[1024,3072]{1,0:T(8,128)(2,1)}, f32[1024,3072]{1,0:T(8,128)}) fusion(f32[3072]{0:T(1024)S(1)} %copy-done.44, bf16[768,3072]{1,0:T(8,128)(2,1)} %all-gather.9.cloned.1.call-done, f32[1024,768]{0,1:T(8,128)S(1)} %get-tuple-element.164, f32[768]{0:T(1024)S(1)} %copy-done.45, f32[768]{0:T(1024)S(1)} %get-tuple-element.115, ...), kind=kOutput, calls=%fused_computation.22 | convolution fusion | flops 4854644736 | bytes 26765312 | tf_op jit(solution)/shard_map/dot_general | solution.py:136
  209.9 53.0 %all-gather.11.cloned.1.call-done = bf16[3072,768]{1,0:T(8,128)(2,1)} async-done(((bf16[96,768]{1,0:T(8,128)(2,1)}), bf16[3072,768]{1,0:T(8,128)(2,1)}) %all-gather.11.cloned.1.call-update) | async-done | bytes 4718608 | tf_op jit(solution)/shard_map/all_gather | solution.py:95
  262.9 9.0 fusion.64
  272.0 1.7 fusion.16
  273.7 2.2 fusion.17
  275.9 3.5 convert_reduce_fusion.2
  279.4 15.4 %convert_reduce_fusion = (f32[3072]{0:T(1024)}, bf16[1024,3072]{1,0:T(8,128)(2,1)S(1)}) fusion(bf16[1024,768]{0,1:T(8,128)(2,1)S(1)} %get-tuple-element.139, bf16[3072,768]{1,0:T(8,128)(2,1)S(1)} %bitcast.120, f32[1024,3072]{1,0:T(8,128)} %get-tuple-element.166, f32[3072]{0:T(1024)S(1)} %copy-done.44), kind=kOutput, calls=%fused_computation.18 | convolution fusion | flops 4882166784 | bytes 25190400 | tf_op jit(solution)/shard_map/td,fd->tf/dot_general | solution.py:154
  294.8 7.1 multiply_reduce_fusion.2
  302.8 1.6 copy-done.12
  305.3 2.8 fusion.65
  308.2 1.4 convolution_convert_fusion
  310.7 13.4 %fusion.4 = f32[12,64,1024]{2,1,0:T(8,128)} fusion(bf16[512,12,64]{0,2,1:T(8,128)(2,1)S(1)} %bitcast.106, f32[12,512]{1,0:T(8,128)S(1)} %log_add_fusion, f32[12,512,1024]{2,1,0:T(8,128)} %get-tuple-element.160, pred[512,1024]{1,0:T(8,128)(4,1)S(1)} %copy-done.8), kind=kOutput, calls=%fused_computation.16 | convolution fusion | flops 830472192 | bytes 29646848 | tf_op jit(solution)/shard_map/hqk,qhe->khe/dot_general | solution.py:191
  324.0 20.2 %multiply_reduce_fusion = (f32[12,512]{1,0:T(8,128)S(1)}, f32[12,512,1024]{2,1,0:T(8,128)}) fusion(f32[12,512]{1,0:T(8,128)S(1)} %log_add_fusion, f32[12,512,1024]{2,1,0:T(8,128)} %get-tuple-element.160, pred[512,1024]{1,0:T(8,128)(4,1)S(1)} %copy-done.8, bf16[512,12,64]{0,2,1:T(8,128)(2,1)S(1)} %bitcast.107, bf16[1024,3,12,64]{0,3,2,1:T(8,128)(2,1)} %bitcast.90), kind=kOutput, calls=%fused_computation.1 | convolution fusion | flops 836757504 | bytes 53264384 | tf_op jit(solution)/shard_map/qhe,khe->hqk/dot_general | solution.py:179
  344.3 20.3 %multiply_reduce_fusion.1 = (f32[12,512]{1,0:T(8,128)S(1)}, f32[12,512,1024]{2,1,0:T(8,128)}) fusion(f32[12,512]{1,0:T(8,128)S(1)} %log_add_fusion.1, f32[12,512,1024]{2,1,0:T(8,128)} %get-tuple-element.162, pred[512,1024]{1,0:T(8,128)(4,1)S(1)} %copy-done.6, bf16[512,12,64]{0,2,1:T(8,128)(2,1)S(1)} %bitcast.104, bf16[1024,3,12,64]{0,3,2,1:T(8,128)(2,1)} %bitcast.91), kind=kOutput, calls=%fused_computation.4 | convolution fusion | flops 836757504 | bytes 53264384 | tf_op jit(solution)/shard_map/qhe,khe->hqk/dot_general | solution.py:179
  364.6 43.0 %multiply_convert_fusion = (bf16[12,512,1024]{2,1,0:T(8,128)(2,1)}, bf16[12,512,1024]{2,1,0:T(8,128)(2,1)}) fusion(f32[12,512,1024]{2,1,0:T(8,128)} %get-tuple-element.173, f32[12,512]{1,0:T(8,128)S(1)} %get-tuple-element.172, f32[12,512]{1,0:T(8,128)S(1)} %log_add_fusion, f32[12,512,1024]{2,1,0:T(8,128)} %get-tuple-element.160, ...), kind=kLoop, calls=%fused_computation | loop fusion | flops 75497472 | bytes 126976000 | tf_op jit(solution)/shard_map/convert_element_type | solution.py:183
  407.6 9.5 %fusion.32 = bf16[512,12,64]{0,2,1:T(8,128)(2,1)} fusion(bf16[12,512,1024]{2,1,0:T(8,128)(2,1)} %get-tuple-element.177, bf16[1024,3,12,64]{0,3,2,1:T(8,128)(2,1)S(1)} %bitcast.99), kind=kOutput, calls=%fused_computation.77 | convolution fusion | flops 806092800 | bytes 14942208 | tf_op jit(solution)/shard_map/hqk,khe->qhe/dot_general | solution.py:186
  417.1 8.6 fusion.40
  425.7 9.2 fusion.33
  434.9 7.5 fusion.29
  442.7 12.4 %fusion.26 = bf16[1024,1,12,64]{0,3,2,1:T(8,128)(2,1)S(1)} fusion(f32[12,64,1024]{2,1,0:T(8,128)S(1)} %copy-done.59, bf16[512,12,64]{0,2,1:T(8,128)(2,1)S(1)} %bitcast.105, f32[12,512]{1,0:T(8,128)S(1)} %log_add_fusion.1, f32[12,512,1024]{2,1,0:T(8,128)} %get-tuple-element.162, pred[512,1024]{1,0:T(8,128)(4,1)S(1)} %copy-done.7), kind=kOutput, calls=%fused_computation.73 | convolution fusion | flops 832045056 | bytes 31219712 | tf_op jit(solution)/shard_map/hqk,qhe->khe/dot_general | solution.py:191
  455.7 2.2 copy-done.9
  458.0 6.0 fusion.41
  464.0 1.8 copy-done.11
  465.8 10.5 %fusion.54 = f32[768,3072]{1,0:T(8,128)} fusion(bf16[1024,3072]{1,0:T(8,128)(2,1)} %copy-done.60, f32[1024,768]{0,1:T(8,128)S(1)} %copy-done.11, f32[768]{0:T(1024)S(1)} %copy-done.46, f32[768]{0:T(1024)S(1)} %get-tuple-element.115, f32[1024]{0:T(1024)S(1)} %fusion.44, f32[1024]{0:T(1024)S(1)} %broadcast_multiply_fusion.1), kind=kOutput, calls=%fused_computation.144 | convolution fusion | flops 4835770368 | bytes 18888704 | tf_op jit(solution)/shard_map/td,tf->df/dot_general | solution.py:158
  476.4 1.3 copy-done.23
  477.7 10.4 %fusion.66 = f32[3072,768]{1,0:T(8,128)} fusion(bf16[1024,3072]{1,0:T(8,128)(2,1)} %get-tuple-element.165, bf16[1024,768]{0,1:T(8,128)(2,1)S(1)} %copy-done.23), kind=kOutput, calls=%fused_computation.154 | convolution fusion | flops 4831838208 | bytes 17301504 | tf_op jit(solution)/shard_map/tf,td->fd/dot_general | solution.py:153
  488.9 2.8 copy.74
  491.7 8.6 multiply_convert_fusion.3
  500.5 2.8 copy.75
  503.3 2.5 convert_reduce_fusion.4
  505.9 40.1 %all-reduce.3 = (f32[2,768]{1,0:T(2,128)S(1)}, f32[7680]{0:T(1024)S(1)}) all-reduce(f32[2,768]{1,0:T(2,128)S(1)} %pad_maximum_fusion.3, f32[7680]{0:T(1024)S(1)} %constant_dynamic-update-slice_fusion), channel_id=6, replica_groups=mesh['dp'=32] {'dp'}, use_global_device_ids=true, to_apply=%region_20.21.clone | all-reduce | flops 9216 | bytes 73728
  547.5 1.6 add_multiply_fusion.4
  549.0 99.9 %reduce-scatter.6.cloned.1.call-done = f32[24,2304]{1,0:T(8,128)} async-done(((f32[768,2304]{1,0:T(8,128)}), f32[24,2304]{1,0:T(8,128)}) %reduce-scatter.6.cloned.1.call-update) | async-done | bytes 221200 | tf_op jit(solution)/shard_map/reduce_scatter | solution.py:219
  648.9 1.8 add_multiply_fusion.3
  650.8 139.4 %reduce-scatter.10.cloned.1.call-done = f32[24,3072]{1,0:T(8,128)} async-done(((f32[768,3072]{1,0:T(8,128)}), f32[24,3072]{1,0:T(8,128)}) %reduce-scatter.10.cloned.1.call-update) | async-done | bytes 294928 | tf_op jit(solution)/shard_map/reduce_scatter | solution.py:221
  790.2 1.9 add_multiply_fusion.2
  792.1 140.1 %reduce-scatter.12.cloned.1.call-done = f32[96,768]{1,0:T(8,128)} async-done(((f32[3072,768]{1,0:T(8,128)}), f32[96,768]{1,0:T(8,128)}) %reduce-scatter.12.cloned.1.call-update) | async-done | bytes 294928 | tf_op jit(solution)/shard_map/reduce_scatter | solution.py:222
  932.2 1.9 add_multiply_fusion.1
  (206 shorter events, 15.5 us)
Async XLA Ops:
  7.2 70.7 %copy-start.17 = (bf16[1024,768]{1,0:T(8,128)(2,1)S(1)}, bf16[1024,768]{1,0:T(8,128)(2,1)}, u32[]{:S(2)}) copy-start(bf16[1024,768]{1,0:T(8,128)(2,1)} %param.27) | copy-start | bytes 4718596
  7.2 77.5 %all-gather.5.cloned.1.call-start = ((), (), s32[]{:S(2)}) async-start(), calls=%async_computation.4 | async-start | bytes 3649536 | tf_op jit(solution)/shard_map/all_gather | solution.py:92
  9.0 171.4 %all-gather.7.cloned.1.call-start = ((), (), s32[]{:S(2)}) async-start(), calls=%async_computation.5 | async-start | bytes 1216512 | tf_op jit(solution)/shard_map/all_gather | solution.py:93
  10.6 186.6 %all-gather.9.cloned.1.call-start = ((), (), s32[]{:S(2)}) async-start(), calls=%async_computation.6 | async-start | bytes 4866048 | tf_op jit(solution)/shard_map/all_gather | solution.py:94
  12.3 250.6 %all-gather.11.cloned.1.call-start = ((), (), s32[]{:S(2)}) async-start(), calls=%async_computation.7 | async-start | bytes 4866048 | tf_op jit(solution)/shard_map/all_gather | solution.py:95
  13.0 12.9 %collective-permute-start = (bf16[2,24]{1,0:T(2,128)(2,1)S(1)}, bf16[2,24]{1,0:T(2,128)(2,1)S(1)}, u32[]{:S(2)}, u32[]{:S(2)}) collective-permute-start(bf16[2,24]{1,0:T(2,128)(2,1)S(1)} %convert_element_type.131), channel_id=1, source_target_pairs={{0,31},{1,0},{2,1},{3,2},{4,3},{5,4},{6,5},{7,6},{8,7},{9,8},{10,9... | collective-permute-start | bytes 296 | tf_op jit(solution)/shard_map/ppermute | solution.py:23
  21.0 526.4 %reduce-scatter.8.cloned.1.call-start = ((), (), s32[]{:S(2)}) async-start(), calls=%async_computation.9 | async-start | bytes 2433024 | tf_op jit(solution)/shard_map/reduce_scatter | solution.py:220
  25.9 139.2 %copy-start.5 = (pred[512,1024]{1,0:T(8,128)(4,1)}, pred[512,1024]{1,0:T(8,128)(4,1)S(1)}, u32[]{:S(2)}) copy-start(pred[512,1024]{1,0:T(8,128)(4,1)S(1)} %get-tuple-element.153) | copy-start | bytes 1572868
  26.0 3.5 collective-permute-start.1
  29.6 40.9 %collective-permute-start.2 = (bf16[2,96]{1,0:T(2,128)(2,1)S(1)}, bf16[2,96]{1,0:T(2,128)(2,1)S(1)}, u32[]{:S(2)}, u32[]{:S(2)}) collective-permute-start(bf16[2,96]{1,0:T(2,128)(2,1)S(1)} %pad_maximum_fusion.6), channel_id=1, source_target_pairs={{0,28},{1,29},{2,30},{3,31},{4,0},{5,1},{6,2},{7,3},{8,4},{9,5},{1... | collective-permute-start | bytes 1160 | tf_op jit(solution)/shard_map/ppermute | solution.py:23
  70.6 3.7 collective-permute-start.3
  74.4 9.5 %collective-permute-start.4 = (bf16[2,384]{1,0:T(2,128)(2,1)S(1)}, bf16[2,384]{1,0:T(2,128)(2,1)S(1)}, u32[]{:S(2)}, u32[]{:S(2)}) collective-permute-start(bf16[2,384]{1,0:T(2,128)(2,1)S(1)} %concatenate.41), channel_id=1, source_target_pairs={{0,16},{1,17},{2,18},{3,19},{4,20},{5,21},{6,22},{7,23},{8,24},{9,... | collective-permute-start | bytes 4616 | tf_op jit(solution)/shard_map/ppermute | solution.py:23
  77.3 103.1 %copy-start.49 = (f32[1,1024]{1,0:T(1,128)}, f32[1,1024]{1,0:T(1,128)S(1)}, u32[]{:S(2)}) copy-start(f32[1,1024]{1,0:T(1,128)S(1)} %convert_element_type.120) | copy-start | bytes 12292
  100.5 26.9 %copy-start.2 = (bf16[1024,2304]{0,1:T(8,128)(2,1)S(1)}, bf16[1024,2304]{0,1:T(8,128)(2,1)}, u32[]{:S(2)}) copy-start(bf16[1024,2304]{0,1:T(8,128)(2,1)} %copy.70) | copy-start | bytes 14155780
  115.1 16.2 %copy-start.1 = (f32[12,512,1024]{2,1,0:T(8,128)S(1)}, f32[12,512,1024]{2,1,0:T(8,128)}, u32[]{:S(2)}) copy-start(f32[12,512,1024]{2,1,0:T(8,128)} %get-tuple-element.160) | copy-start | bytes 75497472
  152.1 15.6 %copy-start = (f32[12,512,1024]{2,1,0:T(8,128)S(1)}, f32[12,512,1024]{2,1,0:T(8,128)}, u32[]{:S(2)}) copy-start(f32[12,512,1024]{2,1,0:T(8,128)} %get-tuple-element.162) | copy-start | bytes 75497472
  184.9 117.0 %copy-start.10 = (f32[1024,768]{0,1:T(8,128)}, f32[1024,768]{0,1:T(8,128)S(1)}, u32[]{:S(2)}) copy-start(f32[1024,768]{0,1:T(8,128)S(1)} %get-tuple-element.164) | copy-start | bytes 9437188
  185.0 12.2 %copy-start.44 = (f32[3072]{0:T(1024)S(1)}, f32[3072]{0:T(1024)}, u32[]{:S(2)}) copy-start(f32[3072]{0:T(1024)} %slice.120) | copy-start | bytes 36868
  185.0 12.2 %copy-start.45 = (f32[768]{0:T(1024)S(1)}, f32[768]{0:T(1024)}, u32[]{:S(2)}) copy-start(f32[768]{0:T(1024)} %get-tuple-element.149) | copy-start | bytes 9220
  197.1 65.8 %copy-start.47 = (f32[768]{0:T(1024)S(1)}, f32[768]{0:T(1024)}, u32[]{:S(2)}) copy-start(f32[768]{0:T(1024)} %get-tuple-element.148) | copy-start | bytes 9220
  262.9 9.1 copy-start.4
  262.9 9.1 copy-start.37
  272.0 7.4 slice-start.4
  273.7 5.7 slice-start.5
  275.9 18.9 %slice-start.2 = ((s8[4718592]{0:T(1024)(128)(4,1)}), s8[4194304]{0:T(1024)(128)(4,1)S(1)}, s32[]{:S(2)}) async-start(s8[4718592]{0:T(1024)(128)(4,1)} %bitcast.117), calls=%async_computation.14 | async-start | bytes 8388608
  279.4 15.4 %copy-start.22 = (bf16[1024,768]{0,1:T(8,128)(2,1)}, bf16[1024,768]{0,1:T(8,128)(2,1)S(1)}, u32[]{:S(2)}) copy-start(bf16[1024,768]{0,1:T(8,128)(2,1)S(1)} %get-tuple-element.139) | copy-start | bytes 4718596
  279.4 15.4 %slice-start.3 = ((s8[4718592]{0:T(1024)(128)(4,1)}), s8[524288]{0:T(1024)(128)(4,1)S(1)}, s32[]{:S(2)}) async-start(s8[4718592]{0:T(1024)(128)(4,1)} %bitcast.117), calls=%async_computation.15 | async-start | bytes 1048576
  294.8 7.1 copy-start.60
  309.7 34.6 %copy-start.15 = (bf16[512,768]{0,1:T(8,128)(2,1)}, bf16[512,768]{0,1:T(8,128)(2,1)S(1)}, u32[]{:S(2)}) copy-start(bf16[512,768]{0,1:T(8,128)(2,1)S(1)} %get-tuple-element.145) | copy-start | bytes 2359300
  324.0 20.3 %copy-start.6 = (pred[512,1024]{1,0:T(8,128)(4,1)S(1)}, pred[512,1024]{1,0:T(8,128)(4,1)}, u32[]{:S(2)}) copy-start(pred[512,1024]{1,0:T(8,128)(4,1)} %copy-done.5) | copy-start | bytes 1572868
  344.3 63.3 %slice-start = ((s8[4718592]{0:T(1024)(128)(4,1)}), s8[524288]{0:T(1024)(128)(4,1)S(1)}, s32[]{:S(2)}) async-start(s8[4718592]{0:T(1024)(128)(4,1)} %bitcast.97), calls=%async_computation.12 | async-start | bytes 1048576
  364.6 43.0 %slice-start.1 = ((s8[4718592]{0:T(1024)(128)(4,1)}), s8[4194304]{0:T(1024)(128)(4,1)S(1)}, s32[]{:S(2)}) async-start(s8[4718592]{0:T(1024)(128)(4,1)} %bitcast.97), calls=%async_computation.13 | async-start | bytes 8388608
  425.6 223.3 %reduce-scatter.6.cloned.1.call-start = ((), (), s32[]{:S(2)}) async-start(), calls=%async_computation.8 | async-start | bytes 7299072 | tf_op jit(solution)/shard_map/reduce_scatter | solution.py:219
  425.7 9.2 copy-start.3
  434.9 7.6 copy-start.14
  434.9 7.8 copy-start.7
  434.9 7.8 copy-start.16
  434.9 7.8 copy-start.59
  464.0 326.2 %reduce-scatter.10.cloned.1.call-start = ((), (), s32[]{:S(2)}) async-start(), calls=%async_computation.10 | async-start | bytes 9732096 | tf_op jit(solution)/shard_map/reduce_scatter | solution.py:221
  476.4 455.9 %reduce-scatter.12.cloned.1.call-start = ((), (), s32[]{:S(2)}) async-start(), calls=%async_computation.11 | async-start | bytes 9732096 | tf_op jit(solution)/shard_map/reduce_scatter | solution.py:222
  488.2 3.5 copy-start.13
  500.3 5.5 copy-start.41
  500.3 5.5 copy-start.43
  500.3 5.6 copy-start.40
  500.3 5.6 copy-start.51
  500.3 5.6 copy-start.42
  500.3 45.8 %copy-start.52 = (f32[2,24]{1,0:T(2,128)S(1)}, f32[2,24]{1,0:T(2,128)}, u32[]{:S(2)}) copy-start(f32[2,24]{1,0:T(2,128)} %param.32) | copy-start | bytes 580
  500.3 45.8 %copy-start.53 = (f32[2,24]{1,0:T(2,128)S(1)}, f32[2,24]{1,0:T(2,128)}, u32[]{:S(2)}) copy-start(f32[2,24]{1,0:T(2,128)} %param.44) | copy-start | bytes 580
  500.3 45.8 %copy-start.54 = (f32[2,24]{1,0:T(2,128)S(1)}, f32[2,24]{1,0:T(2,128)}, u32[]{:S(2)}) copy-start(f32[2,24]{1,0:T(2,128)} %param.38) | copy-start | bytes 580
  500.4 46.4 %copy-start.55 = (f32[240]{0:T(256)S(1)}, f32[240]{0:T(256)}, u32[]{:S(2)}) copy-start(f32[240]{0:T(256)} %param.33) | copy-start | bytes 2884
  500.4 46.4 %copy-start.56 = (f32[240]{0:T(256)S(1)}, f32[240]{0:T(256)}, u32[]{:S(2)}) copy-start(f32[240]{0:T(256)} %param.45) | copy-start | bytes 2884
  500.4 46.4 %copy-start.57 = (f32[240]{0:T(256)S(1)}, f32[240]{0:T(256)}, u32[]{:S(2)}) copy-start(f32[240]{0:T(256)} %param.39) | copy-start | bytes 2884
  500.4 47.1 %copy-start.27 = (f32[24,768]{1,0:T(8,128)S(1)}, f32[24,768]{1,0:T(8,128)}, u32[]{:S(2)}) copy-start(f32[24,768]{1,0:T(8,128)} %param.29) | copy-start | bytes 221188
  500.4 47.0 %copy-start.35 = (f32[24,768]{1,0:T(8,128)S(1)}, f32[24,768]{1,0:T(8,128)}, u32[]{:S(2)}) copy-start(f32[24,768]{1,0:T(8,128)} %param.41) | copy-start | bytes 221188
  500.4 47.0 %copy-start.36 = (f32[24,768]{1,0:T(8,128)S(1)}, f32[24,768]{1,0:T(8,128)}, u32[]{:S(2)}) copy-start(f32[24,768]{1,0:T(8,128)} %param.35) | copy-start | bytes 221188
  500.4 148.5 %copy-start.26 = (f32[24,2304]{1,0:T(8,128)S(1)}, f32[24,2304]{1,0:T(8,128)}, u32[]{:S(2)}) copy-start(f32[24,2304]{1,0:T(8,128)} %param.28) | copy-start | bytes 663556
  500.4 148.5 %copy-start.32 = (f32[24,2304]{1,0:T(8,128)S(1)}, f32[24,2304]{1,0:T(8,128)}, u32[]{:S(2)}) copy-start(f32[24,2304]{1,0:T(8,128)} %param.40) | copy-start | bytes 663556
  500.4 148.5 %copy-start.33 = (f32[24,2304]{1,0:T(8,128)S(1)}, f32[24,2304]{1,0:T(8,128)}, u32[]{:S(2)}) copy-start(f32[24,2304]{1,0:T(8,128)} %param.34) | copy-start | bytes 663556
  503.2 286.9 %copy-start.24 = (f32[24,3072]{1,0:T(8,128)S(1)}, f32[24,3072]{1,0:T(8,128)}, u32[]{:S(2)}) copy-start(f32[24,3072]{1,0:T(8,128)} %param.30) | copy-start | bytes 884740
  503.2 286.9 %copy-start.28 = (f32[24,3072]{1,0:T(8,128)S(1)}, f32[24,3072]{1,0:T(8,128)}, u32[]{:S(2)}) copy-start(f32[24,3072]{1,0:T(8,128)} %param.42) | copy-start | bytes 884740
  503.2 286.9 %copy-start.29 = (f32[24,3072]{1,0:T(8,128)S(1)}, f32[24,3072]{1,0:T(8,128)}, u32[]{:S(2)}) copy-start(f32[24,3072]{1,0:T(8,128)} %param.36) | copy-start | bytes 884740
  503.2 429.0 %copy-start.25 = (f32[96,768]{1,0:T(8,128)S(1)}, f32[96,768]{1,0:T(8,128)}, u32[]{:S(2)}) copy-start(f32[96,768]{1,0:T(8,128)} %param.31) | copy-start | bytes 884740
  503.3 429.0 %copy-start.30 = (f32[96,768]{1,0:T(8,128)S(1)}, f32[96,768]{1,0:T(8,128)}, u32[]{:S(2)}) copy-start(f32[96,768]{1,0:T(8,128)} %param.43) | copy-start | bytes 884740
  503.3 429.0 %copy-start.31 = (f32[96,768]{1,0:T(8,128)S(1)}, f32[96,768]{1,0:T(8,128)}, u32[]{:S(2)}) copy-start(f32[96,768]{1,0:T(8,128)} %param.37) | copy-start | bytes 884740
  (16 other events, 31.3 us)
Sparse Core Ops, SparseCore 0:
  11.5 63.1 all-gather.4
  78.2 52.8 all-gather.6
  134.5 62.5 all-gather.8
  200.5 62.4 all-gather.10
  425.8 97.8 reduce-scatter.7
  530.7 118.1 reduce-scatter.5
  655.4 134.7 reduce-scatter.9
  797.6 134.5 reduce-scatter.11
